TPU v7x, 32 devices: a whole 2x2x4 slice. The times are simulated.
32 devices in a mesh: parts: 2 (over y), tensor: 4 (over z), dp: 4 (over x, core).
Axes of the slice: x: 2, y: 2, z: 4, core: 2. Of those that a mesh axis runs over, the one named last changes fastest.
Arguments:
- inputs: bfloat16 [4096, 8192], P(('parts', 'dp'), 'tensor'), parts along dimension 0, may hold values from -6 to 6
- cotangent: bfloat16 [4096, 8192], P(('parts', 'dp'), 'tensor'), parts along dimension 0, may hold values from -6 to 6
- weight: bfloat16 [8192, 8192], P(None, 'tensor'), may hold values from -0.0625 to 0.0625
- down_weight_maps: bfloat16 [8192, 2048], P('tensor', 'parts'), parts along dimension 1, may hold values from -0.0625 to 0.0625
- up_weight_maps: bfloat16 [2048, 8192], P('parts', 'tensor'), parts along dimension 0, may hold values from -0.75 to 0.75
- counts: int32 [8, 16], P('parts'), parts along dimension 0, may hold values from 0 to 256, as said below
- ranks: int32 [32], P('parts'), parts along dimension 0, may hold values from 8 to 64, as said below
- owners: int32 [32], P('parts'), parts along dimension 0, may hold values from 0 to 3
Outputs:
- projected: bfloat16 [4096, 8192], P(('parts', 'dp'), 'tensor'), parts along dimension 0
- input_grad: bfloat16 [4096, 8192], P(('parts', 'dp'), 'tensor'), parts along dimension 0
- grad_a: float32 [8, 8192, 1024], P(('parts', 'dp'), 'tensor'), parts along dimension 0
- grad_b: float32 [8, 1024, 8192], P(('parts', 'dp'), None, 'tensor'), parts along dimension 0
There are 2 independent parts, one for each index of `parts`. A program takes and returns all parts, laid end to end along the dimension named above; an argument that names none is the same for every part. Nothing has to cross between parts.
Inputs may be any that keep to these rules, and one draw needn't show every extreme that they name: `counts`: each row sums to at most 512, one row to exactly 512, and all rows together to exactly 1024; some entry is exactly 256. `ranks`: each rank is 64 divided by 1, 2, 4 or 8; some trial has 64 and some 64 // 8.
All inputs are finite; a program needn't handle non-finite values.
Results may differ from a plain program's by a relative error of at most 0.0034.
Values may be sent and summed in bfloat16 or wider, within the bound.
A program may use at most 256 MiB of HBM per device.

v0:
```python
import jax
import jax.numpy as jnp
from jax import lax
from jax.sharding import PartitionSpec as P

LARGEST_RANK = 64
TRIALS = 16
LANES = 128
adapter_alpha = 16.0
TRAILING = (((1,), (1,)), ((), ()))
FIRST = (((0,), (0,)), ((), ()))


def fold_columns(values, match):
    width = values.shape[1]
    kept = jnp.where(match, values, 0.0)
    return sum((kept[:, i : i + LANES] for i in range(0, width, LANES)))


def spread_columns(folded, match):
    repeats = match.shape[1] // LANES
    return jnp.where(
        match, jnp.concatenate([folded] * repeats, axis=1), jnp.zeros((), folded.dtype)
    )


def local(inputs, cotangent, weight, down_weight_maps, up_weight_maps, counts, ranks, owners):
    slot_count, feature_local = inputs.shape
    group_count = counts.shape[0]
    width = down_weight_maps.shape[1]
    column = jnp.arange(width, dtype=jnp.int32)
    col_trial = column // LARGEST_RANK
    column_slot = column % LARGEST_RANK
    trial_ids = jnp.arange(TRIALS, dtype=jnp.int32)
    matches = col_trial[:, None] == trial_ids[None, :]
    rank_per_column = jnp.sum(jnp.where(matches, ranks[None, :], 0), axis=1)
    owner_col = jnp.sum(jnp.where(matches, owners[None, :], 0), axis=1)
    scale_per_column = jnp.where(
        column_slot < rank_per_column, adapter_alpha / rank_per_column.astype(jnp.float32), 0.0
    )
    trial_rows = jnp.sum(counts, axis=0)
    per_trial = 1.0 / jnp.maximum(trial_rows, 1).astype(jnp.float32)
    inverse_col = jnp.sum(jnp.where(matches, per_trial[None, :], 0.0), axis=1)
    cumulative = jnp.cumsum(counts, axis=1)
    group_ids = jnp.arange(group_count, dtype=jnp.int32)
    my_group = lax.axis_index("dp")
    positions = jnp.arange(slot_count, dtype=jnp.int32)
    trial_all = jnp.sum(
        (positions[None, :, None] >= cumulative[:, None, :]).astype(jnp.int32), axis=2
    )
    row_trial = jnp.sum(jnp.where((group_ids == my_group)[:, None], trial_all, 0), axis=0)
    is_live = row_trial < TRIALS
    match = row_trial[:, None] == col_trial[None, :]
    match_all = trial_all.reshape(-1)[:, None] == col_trial[None, :]
    coef = jnp.where(match, scale_per_column[None, :], 0.0)
    coef_folded = fold_columns(coef, match)
    down_part = jnp.dot(inputs, down_weight_maps, preferred_element_type=jnp.float32)
    back_part = lax.dot_general(
        cotangent, up_weight_maps, TRAILING, preferred_element_type=jnp.float32
    )
    folded = jnp.concatenate(
        [fold_columns(down_part, match), fold_columns(back_part, match)], axis=1
    )
    folded = lax.psum(folded, "tensor")
    scaled_down_f = (coef_folded * folded[:, :LANES]).astype(jnp.bfloat16)
    scaled_back_f = (coef_folded * folded[:, LANES:]).astype(jnp.bfloat16)
    all_inputs = lax.all_gather(inputs, "tensor", axis=1, tiled=True)
    mine = lax.axis_index("tensor")
    block = jnp.arange(weight.shape[0], dtype=jnp.int32) // feature_local
    frozen_back = lax.dot_general(cotangent, weight, TRAILING, preferred_element_type=jnp.float32)
    others = jnp.where((block == mine)[None, :], 0.0, frozen_back).astype(jnp.bfloat16)
    others_share = lax.psum_scatter(others, "tensor", scatter_dimension=1, tiled=True)
    own_weight = lax.dynamic_slice_in_dim(weight, mine * feature_local, feature_local, 0)
    own_share = lax.dot_general(cotangent, own_weight, TRAILING, preferred_element_type=jnp.float32)
    frozen_share = own_share + others_share.astype(jnp.float32)
    group_inputs = lax.all_gather(inputs, "dp", axis=0, tiled=True)
    group_cotangent = lax.all_gather(cotangent, "dp", axis=0, tiled=True)
    both = lax.all_gather(
        jnp.concatenate([scaled_down_f, scaled_back_f], axis=1), "dp", axis=0, tiled=True
    )
    frozen_output = jnp.dot(all_inputs, weight, preferred_element_type=jnp.float32)
    scaled_down = spread_columns(scaled_down_f, match)
    scaled_back = spread_columns(scaled_back_f, match)
    merged = frozen_output + jnp.dot(
        scaled_down, up_weight_maps, preferred_element_type=jnp.float32
    )
    projected = jnp.where(is_live[:, None], merged, 0.0).astype(jnp.bfloat16)
    adapter_in = lax.dot_general(
        scaled_back, down_weight_maps, TRAILING, preferred_element_type=jnp.float32
    )
    input_grad = jnp.where(is_live[:, None], frozen_share + adapter_in, 0.0).astype(jnp.bfloat16)
    owned = jnp.where(owner_col == my_group, inverse_col, 0.0)
    down_all = spread_columns(both[:, :LANES], match_all)
    back_all = spread_columns(both[:, LANES:], match_all)
    grad_a = lax.dot_general(group_inputs, back_all, FIRST, preferred_element_type=jnp.float32)
    grad_b = lax.dot_general(down_all, group_cotangent, FIRST, preferred_element_type=jnp.float32)
    grad_a = (grad_a * owned[None, :])[None]
    grad_b = (grad_b * owned[:, None])[None]
    return (projected, input_grad, grad_a, grad_b)


def solution(mesh):
    return jax.shard_map(
        local,
        mesh=mesh,
        in_specs=(
            P(("parts", "dp"), "tensor"),
            P(("parts", "dp"), "tensor"),
            P(None, "tensor"),
            P("tensor", "parts"),
            P("parts", "tensor"),
            P("parts", None),
            P("parts"),
            P("parts"),
        ),
        out_specs=(
            P(("parts", "dp"), "tensor"),
            P(("parts", "dp"), "tensor"),
            P(("parts", "dp"), "tensor", None),
            P(("parts", "dp"), None, "tensor"),
        ),
        check_vma=False,
    )
```

profile of v0, /device:TPU:0, one launch (start us, length us, event | category | flops | bytes accessed | tf_op | source)
XLA Modules:
  0.0 511.5 jit_solution(14548352022868119628)
XLA Ops:
  8.3 5.3 %compare_select_fusion.4 = f32[512,1024]{1,0:T(8,128)S(1)} fusion(bf16[512,2048]{1,0:T(8,128)(2,1)} %param.9, bf16[1024,2048]{1,0:T(8,128)(2,1)} %param.12, s32[1024]{0:T(1024)S(1)} %add_select_fusion.1, s32[512]{0:T(512)S(1)} %select_reduce_fusion.3), kind=kOutput, calls=%fused_computation.9 | convolution fusion | flops 2148532224 | bytes 8394752 | tf_op jit(solution)/shard_map/dot_general | solution.py:58
  13.8 2.3 compare_select_fusion.5
  17.6 40.7 %all-reduce.2.cloned.1.call-done = f32[512,256]{1,0:T(8,128)} async-done(((f32[512,256]{1,0:T(8,128)}), f32[512,256]{1,0:T(8,128)}) %all-reduce.2.cloned.1.call-update) | async-done | bytes 524304 | tf_op jit(solution)/shard_map/psum | solution.py:64
  58.2 1.1 constant_dynamic-update-slice_fusion.15
  59.3 1.8 constant_dynamic-update-slice_fusion.7
  64.0 24.4 %select_convert_fusion = bf16[512,8192]{1,0:T(8,128)(2,1)} fusion(bf16[512,2048]{1,0:T(8,128)(2,1)S(1)} %copy-done.2, bf16[8192,2048]{1,0:T(8,128)(2,1)} %param.10, pred[8192]{0:T(1024)(128)(4,1)S(1)} %fusion.23), kind=kOutput, calls=%fused_computation | convolution fusion | flops 17188257792 | bytes 44048384 | tf_op jit(solution)/shard_map/dot_general | solution.py:70
  89.6 7.7 %fusion.14 = f32[512,2048]{1,0:T(8,128)} fusion(bf16[2048,1024]{1,0:T(8,128)(2,1)} %param.11, bf16[512,1024]{1,0:T(8,128)(2,1)S(1)} %constant_dynamic-update-slice_fusion.8, s32[1024]{0:T(1024)S(1)} %add_select_fusion.1, s32[512]{0:T(512)S(1)} %select_reduce_fusion.3), kind=kOutput, calls=%fused_computation.25 | convolution fusion | flops 2148532224 | bytes 9443328 | tf_op jit(solution)/shard_map/dot_general | solution.py:88
  97.6 4.4 fusion.13
  102.0 2.0 slice_dynamic-update-slice_fusion.6
  104.0 2.0 slice_dynamic-update-slice_fusion.5
  106.0 1.9 slice_dynamic-update-slice_fusion.4
  107.9 1.9 slice_dynamic-update-slice_fusion.3
  110.6 0.9 slice_dynamic-update-slice_fusion.1
  111.5 0.9 slice_dynamic-update-slice_fusion
  112.4 1.0 slice_dynamic-update-slice_fusion.7
  119.2 19.4 %all-gather.9.cloned.1.call-done = bf16[2048,2048]{1,0:T(8,128)(2,1)} async-done(((bf16[512,2048]{1,0:T(8,128)(2,1)}), bf16[2048,2048]{1,0:T(8,128)(2,1)}) %all-gather.9.cloned.1.call-update) | async-done | bytes 8388624 | tf_op jit(solution)/shard_map/all_gather | solution.py:76
  138.6 14.9 %multiply_bitcast_fusion.1 = f32[1,2048,1024]{1,2,0:T(8,128)} fusion(bf16[2048,2048]{1,0:T(8,128)(2,1)} %all-gather.9.cloned.1.call-done, bf16[2048,1024]{1,0:T(8,128)(2,1)} %slice_dynamic-update-slice_fusion.15, f32[1024]{0:T(1024)S(1)} %compare_select_fusion.12, s32[1024]{0:T(1024)S(1)} %add_select_fusion.1, s32[2048]{0:T(1024)S(1)} %bitcast.30), kind=kOutput, calls=%fused_computation.4 | convolution fusion | flops 8596226048 | bytes 20987904 | tf_op jit(solution)/shard_map/dot_general | solution.py:95
  153.5 9.2 %copy.15 = f32[1,2048,1024]{2,1,0:T(8,128)} copy(f32[1,2048,1024]{1,2,0:T(8,128)} %multiply_bitcast_fusion.1) | data formatting | bytes 16777216
  162.7 35.6 %all-gather.11.cloned.1.call-done = bf16[2048,2048]{1,0:T(8,128)(2,1)} async-done(((bf16[512,2048]{1,0:T(8,128)(2,1)}), bf16[2048,2048]{1,0:T(8,128)(2,1)}) %all-gather.11.cloned.1.call-update) | async-done | bytes 8388624 | tf_op jit(solution)/shard_map/all_gather | solution.py:77
  198.3 14.9 %multiply_bitcast_fusion = f32[1,1024,2048]{2,1,0:T(8,128)} fusion(bf16[2048,2048]{1,0:T(8,128)(2,1)} %all-gather.11.cloned.1.call-done, bf16[2048,1024]{1,0:T(8,128)(2,1)} %get-tuple-element.19, f32[1024]{0:T(1024)S(1)} %compare_select_fusion.12, s32[1024]{0:T(1024)S(1)} %add_select_fusion.1, s32[2048]{0:T(1024)S(1)} %bitcast.31), kind=kOutput, calls=%fused_computation.3 | convolution fusion | flops 8596226048 | bytes 20987904 | tf_op jit(solution)/shard_map/dot_general | solution.py:96
  213.2 136.2 %all-gather.5.cloned.1.call-done = bf16[512,8192]{1,0:T(8,128)(2,1)} async-done(((bf16[512,2048]{1,0:T(8,128)(2,1)}), bf16[512,8192]{1,0:T(8,128)(2,1)}) %all-gather.5.cloned.1.call-update) | async-done | bytes 8388624 | tf_op jit(solution)/shard_map/all_gather | solution.py:67
  349.4 24.9 %select_convert_fusion.1 = bf16[512,2048]{1,0:T(8,128)(2,1)} fusion(f32[512,2048]{1,0:T(8,128)} %fusion.13, bf16[512,8192]{1,0:T(8,128)(2,1)} %all-gather.5.cloned.1.call-done, bf16[8192,2048]{1,0:T(8,128)(2,1)} %param.10, pred[512]{0:T(512)(128)(4,1)S(1)} %broadcast_compare_fusion), kind=kOutput, calls=%fused_computation.19 | convolution fusion | flops 17183014912 | bytes 48235008 | tf_op jit(solution)/shard_map/dot_general | solution.py:81
  374.3 120.0 %reduce-scatter.2.cloned.1.call-done = bf16[512,2048]{1,0:T(8,128)(2,1)} async-done(((bf16[512,8192]{1,0:T(8,128)(2,1)}), bf16[512,2048]{1,0:T(8,128)(2,1)}) %reduce-scatter.2.cloned.1.call-update) | async-done | bytes 2097168 | tf_op jit(solution)/shard_map/reduce_scatter | solution.py:72
  494.3 10.3 %fusion.4 = bf16[512,2048]{1,0:T(8,128)(2,1)} fusion(f32[512,2048]{1,0:T(8,128)} %fusion.14, bf16[512,2048]{1,0:T(8,128)(2,1)} %reduce-scatter.2.cloned.1.call-done, bf16[512,2048]{1,0:T(8,128)(2,1)S(1)} %copy-done.2, bf16[8192,2048]{1,0:T(8,128)(2,1)} %param.10, s32[]{:T(128)S(6)} %select_n.128, pred[512]{0:T(512)(128)(4,1)S(1)} %broadcast_compare_fusion), kind=kOutput, calls=%fused_computation.16 | convolution fusion | flops 4300210176 | bytes 18874884 | tf_op jit(solution)/shard_map/dot_general | solution.py:74
  (72 shorter events, 13.4 us)
Async XLA Ops:
  7.2 51.1 %all-reduce.2.cloned.1.call-start = ((), (), s32[]{:S(2)}) async-start(), calls=%async_computation.2 | async-start | bytes 1048576 | tf_op jit(solution)/shard_map/psum | solution.py:64
  8.3 5.5 %copy-start.1 = (bf16[512,2048]{1,0:T(8,128)(2,1)S(1)}, bf16[512,2048]{1,0:T(8,128)(2,1)}, u32[]{:S(2)}) copy-start(bf16[512,2048]{1,0:T(8,128)(2,1)} %param.8) | copy-start | bytes 6291460
  8.3 5.5 %copy-start.7 = (bf16[2048,1024]{1,0:T(8,128)(2,1)S(1)}, bf16[2048,1024]{1,0:T(8,128)(2,1)}, u32[]{:S(2)}) copy-start(bf16[2048,1024]{1,0:T(8,128)(2,1)} %param.11) | copy-start | bytes 12582916
  13.8 3.4 copy-start.5
  13.8 3.4 copy-start.6
  17.1 84.9 %all-gather.7.cloned.1.call-start = ((), (), s32[]{:S(2)}) async-start(), calls=%async_computation.4 | async-start | bytes 1310720 | tf_op jit(solution)/shard_map/all_gather | solution.py:78
  59.3 4.7 copy-start.2
  61.8 76.8 %all-gather.9.cloned.1.call-start = ((), (), s32[]{:S(2)}) async-start(), calls=%async_computation.5 | async-start | bytes 10485760 | tf_op jit(solution)/shard_map/all_gather | solution.py:76
  62.6 135.8 %all-gather.11.cloned.1.call-start = ((), (), s32[]{:S(2)}) async-start(), calls=%async_computation.6 | async-start | bytes 10485760 | tf_op jit(solution)/shard_map/all_gather | solution.py:77
  63.2 286.3 %all-gather.5.cloned.1.call-start = ((), (), s32[]{:S(2)}) async-start(), calls=%async_computation.1 | async-start | bytes 10485760 | tf_op jit(solution)/shard_map/all_gather | solution.py:67
  63.8 430.6 %reduce-scatter.2.cloned.1.call-start = ((), (), s32[]{:S(2)}) async-start(), calls=%async_computation.3 | async-start | bytes 10485760 | tf_op jit(solution)/shard_map/reduce_scatter | solution.py:72
  88.4 0.7 copy-start.4
  89.5 7.7 %copy-start.3 = (bf16[512,1024]{1,0:T(8,128)(2,1)S(1)}, bf16[512,1024]{1,0:T(8,128)(2,1)}, u32[]{:S(2)}) copy-start(bf16[512,1024]{1,0:T(8,128)(2,1)} %get-tuple-element.17) | copy-start | bytes 3145732
  89.5 8.0 %copy-start.8 = (bf16[1024,2048]{1,0:T(8,128)(2,1)S(1)}, bf16[1024,2048]{1,0:T(8,128)(2,1)}, u32[]{:S(2)}) copy-start(bf16[1024,2048]{1,0:T(8,128)(2,1)} %param.12) | copy-start | bytes 12582916
  102.0 7.8 %copy-start = (bf16[2048,256]{1,0:T(8,128)(2,1)S(1)}, bf16[2048,256]{1,0:T(8,128)(2,1)}, u32[]{:S(2)}) copy-start(bf16[2048,256]{1,0:T(8,128)(2,1)} %all-gather.7.cloned.1.call-done) | copy-start | bytes 3145732
Sparse Core Ops, SparseCore 0:
  17.2 40.9 all-reduce.1
  62.0 16.6 all-gather.6
  80.3 58.2 all-gather.8
  140.0 58.2 all-gather.10
  199.8 149.6 all-gather.4
  351.6 142.6 reduce-scatter.1
where the time goes:
time: 512 us; the launch traced here: 511 us
  waiting for transfers between devices  354 us (69%)
  matrix products  109 us (21%)
  local copies, waits for them, and re-layouts  27.7 us (5%)
  between operations  14.4 us (3%)
  other arithmetic  6.18 us (1%)
    all_gather x1, waiting for transfers between devices, local(): all_inputs = lax.all_gather(inputs, 'tensor', axis=1, tiled=True)  136 us
    reduce_scatter x1, waiting for transfers between devices, local(): lax.psum_scatter(others, 'tensor', scatter_dimension=1, tiled=True)  120 us
    psum x1, waiting for transfers between devices, local(): folded = lax.psum(folded, 'tensor')  40.7 us
    all_gather x1, waiting for transfers between devices, local(): group_cotangent = lax.all_gather(cotangent, 'dp', axis=0, tiled=True)  35.6 us
    unnamed x45, local copies, waits for them, and re-layouts  25.8 us
    dot_general x1, matrix products, local(): jnp.dot(all_inputs, weight, preferred_element_type=jnp.float32)  24.9 us
    dot_general x1, matrix products, local(): lax.dot_general(cotangent, weight, TRAILING, preferred_element_type=jnp.f...  24.4 us
    all_gather x1, waiting for transfers between devices, local(): group_inputs = lax.all_gather(inputs, 'dp', axis=0, tiled=True)  19.4 us
  transfers between devices with their start and end apart: 6, of which 5 were waited for; matrix products, arithmetic and copies ran while one was open for 23% of the time, Pallas kernels for 0%

commit v1 on v0

--- a/solution.py
+++ b/solution.py
@@ -73,7 +73,12 @@
     own_weight = lax.dynamic_slice_in_dim(weight, mine * feature_local, feature_local, 0)
     own_share = lax.dot_general(cotangent, own_weight, TRAILING, preferred_element_type=jnp.float32)
     frozen_share = own_share + others_share.astype(jnp.float32)
-    group_inputs = lax.all_gather(inputs, "dp", axis=0, tiled=True)
+    ring = [inputs]
+    for hop in range(3):
+        ring.append(lax.ppermute(ring[-1], "dp", [(dev, (dev + 1) % 4) for dev in range(4)]))
+    group_inputs = jnp.roll(
+        jnp.concatenate(ring[::-1], axis=0), (lax.axis_index("dp") + 1) * ring[0].shape[0], axis=0
+    )
     group_cotangent = lax.all_gather(cotangent, "dp", axis=0, tiled=True)
     both = lax.all_gather(
         jnp.concatenate([scaled_down_f, scaled_back_f], axis=1), "dp", axis=0, tiled=True

time: 512 us -> 471 us (0.920)
  waiting for transfers between devices: 354 us -> 320 us
  local copies, waits for them, and re-layouts: 27.7 us -> 20.1 us
    ppermute x0 -> x3, waiting for transfers between devices: none -> 73.3 us  [local(): lax.ppermute(ring[-1], 'dp', [(dev, (dev + 1) % 4) for dev in range(4)])]
    all_gather x1, waiting for transfers between devices: 136 us -> 85.7 us  [local(): all_inputs = lax.all_gather(inputs, 'tensor', axis=1, tiled=True)]
    all_gather x1, waiting for transfers between devices: 35.6 us -> 0.01 us  [local(): group_cotangent = lax.all_gather(cotangent, 'dp', axis=0, tiled=True)]
    all_gather x1 -> x0, waiting for transfers between devices: 19.4 us -> none  [local(): group_inputs = lax.all_gather(inputs, 'dp', axis=0, tiled=True)]
    unnamed x45 -> x53, local copies, waits for them, and re-layouts: 25.8 us -> 18.8 us
  transfers between devices with their start and end apart: 6 -> 8, of which waited for: 5 -> 5; matrix products, arithmetic and copies ran while one was open for 23% -> 23% of each run, Pallas kernels for 0% -> 0%
where the time goes in v1:
time: 471 us; the launch traced here: 470 us
  waiting for transfers between devices  320 us (68%)
  matrix products  106 us (23%)
  local copies, waits for them, and re-layouts  20.1 us (4%)
  between operations  14.2 us (3%)
  other arithmetic  8.02 us (2%)
    reduce_scatter x1, waiting for transfers between devices, local(): lax.psum_scatter(others, 'tensor', scatter_dimension=1, tiled=True)  120 us
    all_gather x1, waiting for transfers between devices, local(): all_inputs = lax.all_gather(inputs, 'tensor', axis=1, tiled=True)  85.7 us
    ppermute x3, waiting for transfers between devices, local(): lax.ppermute(ring[-1], 'dp', [(dev, (dev + 1) % 4) for dev in range(4)])  73.3 us
    psum x1, waiting for transfers between devices, local(): folded = lax.psum(folded, 'tensor')  39.4 us
    dot_general x1, matrix products, local(): lax.dot_general(cotangent, weight, TRAILING, preferred_element_type=jnp.f...  25 us
    dot_general x1, matrix products, local(): jnp.dot(all_inputs, weight, preferred_element_type=jnp.float32)  24.9 us
    unnamed x53, local copies, waits for them, and re-layouts  18.8 us
    dot_general x1, matrix products, local(): lax.dot_general(down_all, group_cotangent, FIRST, preferred_element_type=...  14.9 us
  transfers between devices with their start and end apart: 8, of which 5 were waited for; matrix products, arithmetic and copies ran while one was open for 23% of the time, Pallas kernels for 0%

profile of v1, /device:TPU:0, one launch (start us, length us, event | category | flops | bytes accessed | tf_op | source)
XLA Modules:
  0.0 470.2 jit_solution(5923374684088605973)
XLA Ops:
  8.3 5.3 %compare_select_fusion.4 = f32[512,1024]{1,0:T(8,128)S(1)} fusion(bf16[512,2048]{1,0:T(8,128)(2,1)} %param.9, bf16[1024,2048]{1,0:T(8,128)(2,1)} %param.12, s32[1024]{0:T(1024)S(1)} %add_select_fusion.1, s32[512]{0:T(512)S(1)} %select_reduce_fusion.3), kind=kOutput, calls=%fused_computation.11 | convolution fusion | flops 2148532224 | bytes 8394752 | tf_op jit(solution)/shard_map/dot_general | solution.py:58
  13.8 2.3 compare_select_fusion.5
  17.3 1.6 compare_select_fusion.6
  18.9 39.4 %all-reduce.2.cloned.1.call-done = f32[512,256]{1,0:T(8,128)} async-done(((f32[512,256]{1,0:T(8,128)}), f32[512,256]{1,0:T(8,128)}) %all-reduce.2.cloned.1.call-update) | async-done | bytes 524304 | tf_op jit(solution)/shard_map/psum | solution.py:64
  58.2 1.7 constant_dynamic-update-slice_fusion.15
  60.0 1.6 constant_dynamic-update-slice_fusion.7
  64.0 25.0 %select_convert_fusion = bf16[512,8192]{1,0:T(8,128)(2,1)} fusion(bf16[512,2048]{1,0:T(8,128)(2,1)} %param.9, bf16[8192,2048]{1,0:T(8,128)(2,1)} %param.10, pred[8192]{0:T(1024)(128)(4,1)S(1)} %fusion.27), kind=kOutput, calls=%fused_computation | convolution fusion | flops 17188257792 | bytes 44048384 | tf_op jit(solution)/shard_map/dot_general | solution.py:70
  94.8 7.3 %fusion.17 = f32[512,2048]{1,0:T(8,128)} fusion(bf16[1024,2048]{1,0:T(8,128)(2,1)} %param.12, bf16[512,1024]{1,0:T(8,128)(2,1)} %constant_dynamic-update-slice_fusion, s32[1024]{0:T(1024)S(1)} %add_select_fusion.1, s32[512]{0:T(512)S(1)} %select_reduce_fusion.3), kind=kOutput, calls=%fused_computation.26 | convolution fusion | flops 2148532224 | bytes 9443328 | tf_op jit(solution)/shard_map/dot_general | solution.py:89
  102.1 4.4 fusion.18
  106.6 1.4 collective-permute-start.1
  108.0 1.3 slice_dynamic-update-slice_fusion.6
  111.7 1.2 slice_dynamic-update-slice_fusion.3
  114.2 48.6 %collective-permute-done.1 = bf16[512,2048]{1,0:T(8,128)(2,1)} collective-permute-done((bf16[512,2048]{1,0:T(8,128)(2,1)}, bf16[512,2048]{1,0:T(8,128)(2,1)}, u32[]{:S(2)}, u32[]{:S(2)}) %collective-permute-start.1) | collective-permute-done | bytes 2097184 | tf_op jit(solution)/shard_map/ppermute | solution.py:78
  163.7 24.7 %collective-permute-done.2 = bf16[512,2048]{1,0:T(8,128)(2,1)S(1)} collective-permute-done((bf16[512,2048]{1,0:T(8,128)(2,1)}, bf16[512,2048]{1,0:T(8,128)(2,1)S(1)}, u32[]{:S(2)}, u32[]{:S(2)}) %collective-permute-start.2) | collective-permute-done | bytes 2097184 | tf_op jit(solution)/shard_map/ppermute | solution.py:78
  188.6 1.7 constant_dynamic-update-slice_fusion.22
  190.3 1.7 constant_dynamic-update-slice_fusion.21
  192.4 1.7 constant_dynamic-update-slice_fusion.18
  194.1 1.7 constant_dynamic-update-slice_fusion.17
  196.0 11.8 %multiply_bitcast_fusion.1 = f32[1,2048,1024]{2,1,0:T(8,128)} fusion(bf16[4096,2048]{1,0:T(8,128)(2,1)S(1)} %constant_dynamic-update-slice_fusion.16, s32[]{:T(128)S(6)} %select_n.146, bf16[2048,1024]{1,0:T(8,128)(2,1)S(1)} %slice_dynamic-update-slice_fusion.15, f32[1024]{0:T(1024)S(1)} %compare_select_fusion.12, s32[1024]{0:T(1024)S(1)} %add_select_fusion.1, ...), kind=kOutput, calls=%fused_computation.4 | convolution fusion | flops 8596226048 | bytes 20987908 | tf_op jit(solution)/shard_map/dot_general | solution.py:100
  207.8 14.9 %multiply_bitcast_fusion = f32[1,1024,2048]{2,1,0:T(8,128)} fusion(bf16[2048,2048]{1,0:T(8,128)(2,1)} %all-gather.8.cloned.1.call-done, bf16[2048,1024]{1,0:T(8,128)(2,1)} %copy-done.4, f32[1024]{0:T(1024)S(1)} %compare_select_fusion.12, s32[1024]{0:T(1024)S(1)} %add_select_fusion.1, s32[2048]{0:T(1024)S(1)} %bitcast.28), kind=kOutput, calls=%fused_computation.3 | convolution fusion | flops 8596226048 | bytes 20987904 | tf_op jit(solution)/shard_map/dot_general | solution.py:101
  222.7 85.7 %all-gather.4.cloned.1.call-done = bf16[512,8192]{1,0:T(8,128)(2,1)} async-done(((bf16[512,2048]{1,0:T(8,128)(2,1)}), bf16[512,8192]{1,0:T(8,128)(2,1)}) %all-gather.4.cloned.1.call-update) | async-done | bytes 8388624 | tf_op jit(solution)/shard_map/all_gather | solution.py:67
  308.5 24.9 %select_convert_fusion.1 = bf16[512,2048]{1,0:T(8,128)(2,1)} fusion(f32[512,2048]{1,0:T(8,128)} %fusion.17, bf16[512,8192]{1,0:T(8,128)(2,1)} %all-gather.4.cloned.1.call-done, bf16[8192,2048]{1,0:T(8,128)(2,1)} %param.10, pred[512]{0:T(512)(128)(4,1)S(1)} %broadcast_compare_fusion), kind=kOutput, calls=%fused_computation.21 | convolution fusion | flops 17183014912 | bytes 48235008 | tf_op jit(solution)/shard_map/dot_general | solution.py:86
  333.4 120.0 %reduce-scatter.2.cloned.1.call-done = bf16[512,2048]{1,0:T(8,128)(2,1)} async-done(((bf16[512,8192]{1,0:T(8,128)(2,1)}), bf16[512,2048]{1,0:T(8,128)(2,1)}) %reduce-scatter.2.cloned.1.call-update) | async-done | bytes 2097168 | tf_op jit(solution)/shard_map/reduce_scatter | solution.py:72
  453.4 10.3 %fusion.8 = bf16[512,2048]{1,0:T(8,128)(2,1)} fusion(f32[512,2048]{1,0:T(8,128)} %fusion.18, bf16[512,2048]{1,0:T(8,128)(2,1)} %reduce-scatter.2.cloned.1.call-done, bf16[512,2048]{1,0:T(8,128)(2,1)S(1)} %copy-done.3, bf16[8192,2048]{1,0:T(8,128)(2,1)} %param.10, s32[]{:T(128)S(6)} %select_n.140, pred[512]{0:T(512)(128)(4,1)S(1)} %broadcast_compare_fusion), kind=kOutput, calls=%fused_computation.18 | convolution fusion | flops 4300210176 | bytes 18874884 | tf_op jit(solution)/shard_map/dot_general | solution.py:74
  (84 shorter events, 15.4 us)
Async XLA Ops:
  7.2 51.1 %all-reduce.2.cloned.1.call-start = ((), (), s32[]{:S(2)}) async-start(), calls=%async_computation.2 | async-start | bytes 1048576 | tf_op jit(solution)/shard_map/psum | solution.py:64
  8.3 5.5 %copy-start.1 = (bf16[512,2048]{1,0:T(8,128)(2,1)S(1)}, bf16[512,2048]{1,0:T(8,128)(2,1)}, u32[]{:S(2)}) copy-start(bf16[512,2048]{1,0:T(8,128)(2,1)} %param.8) | copy-start | bytes 6291460
  8.3 5.5 %copy-start.8 = (bf16[2048,1024]{1,0:T(8,128)(2,1)S(1)}, bf16[2048,1024]{1,0:T(8,128)(2,1)}, u32[]{:S(2)}) copy-start(bf16[2048,1024]{1,0:T(8,128)(2,1)} %param.11) | copy-start | bytes 12582916
  13.8 3.4 copy-start.6
  13.8 3.4 copy-start.7
  17.1 90.9 %all-gather.6.cloned.1.call-start = ((), (), s32[]{:S(2)}) async-start(), calls=%async_computation.4 | async-start | bytes 1310720 | tf_op jit(solution)/shard_map/all_gather | solution.py:83
  18.9 44.9 %copy-start.2 = (bf16[512,2048]{1,0:T(8,128)(2,1)S(1)}, bf16[512,2048]{1,0:T(8,128)(2,1)}, u32[]{:S(2)}) copy-start(bf16[512,2048]{1,0:T(8,128)(2,1)} %param.8) | copy-start | bytes 6291460
  62.4 145.4 %all-gather.8.cloned.1.call-start = ((), (), s32[]{:S(2)}) async-start(), calls=%async_computation.5 | async-start | bytes 10485760 | tf_op jit(solution)/shard_map/all_gather | solution.py:82
  63.1 245.4 %all-gather.4.cloned.1.call-start = ((), (), s32[]{:S(2)}) async-start(), calls=%async_computation.1 | async-start | bytes 10485760 | tf_op jit(solution)/shard_map/all_gather | solution.py:67
  63.7 389.7 %reduce-scatter.2.cloned.1.call-start = ((), (), s32[]{:S(2)}) async-start(), calls=%async_computation.3 | async-start | bytes 10485760 | tf_op jit(solution)/shard_map/reduce_scatter | solution.py:72
  63.7 42.8 %collective-permute-start = (bf16[512,2048]{1,0:T(8,128)(2,1)S(1)}, bf16[512,2048]{1,0:T(8,128)(2,1)}, u32[]{:S(2)}, u32[]{:S(2)}) collective-permute-start(bf16[512,2048]{1,0:T(8,128)(2,1)S(1)} %copy-done.2), channel_id=1, source_target_pairs={{0,1},{1,2},{2,3},{3,0},{4,5},{5,6},{6,7},{7,4},{8,9},{9,10},{10,1... | collective-permute-start | bytes 6291464 | tf_op jit(solution)/shard_map/ppermute | solution.py:78
  89.0 0.7 copy-start.5
  94.8 7.3 %copy-start.9 = (bf16[2048,1024]{1,0:T(8,128)(2,1)S(1)}, bf16[2048,1024]{1,0:T(8,128)(2,1)}, u32[]{:S(2)}) copy-start(bf16[2048,1024]{1,0:T(8,128)(2,1)} %param.11) | copy-start | bytes 12582916
  106.6 56.2 %collective-permute-start.1 = (bf16[512,2048]{1,0:T(8,128)(2,1)}, bf16[512,2048]{1,0:T(8,128)(2,1)}, u32[]{:S(2)}, u32[]{:S(2)}) collective-permute-start(bf16[512,2048]{1,0:T(8,128)(2,1)} %collective-permute-done), channel_id=1, source_target_pairs={{0,1},{1,2},{2,3},{3,0},{4,5},{5,6},{6,7},{7,4},{8,9},{9,10},{10,1... | collective-permute-start | bytes 6291464 | tf_op jit(solution)/shard_map/ppermute | solution.py:78
  108.0 5.0 %copy-start = (bf16[2048,256]{1,0:T(8,128)(2,1)S(1)}, bf16[2048,256]{1,0:T(8,128)(2,1)}, u32[]{:S(2)}) copy-start(bf16[2048,256]{1,0:T(8,128)(2,1)} %all-gather.6.cloned.1.call-done) | copy-start | bytes 3145732
  113.8 49.9 %copy-start.4 = (bf16[2048,1024]{1,0:T(8,128)(2,1)}, bf16[2048,1024]{1,0:T(8,128)(2,1)S(1)}, u32[]{:S(2)}) copy-start(bf16[2048,1024]{1,0:T(8,128)(2,1)S(1)} %get-tuple-element.11) | copy-start | bytes 12582916
  162.8 25.7 %collective-permute-start.2 = (bf16[512,2048]{1,0:T(8,128)(2,1)}, bf16[512,2048]{1,0:T(8,128)(2,1)S(1)}, u32[]{:S(2)}, u32[]{:S(2)}) collective-permute-start(bf16[512,2048]{1,0:T(8,128)(2,1)} %collective-permute-done.1), channel_id=1, source_target_pairs={{0,1},{1,2},{2,3},{3,0},{4,5},{5,6},{6,7},{7,4},{8,9},{9,10},{10,1... | collective-permute-start | bytes 6291464 | tf_op jit(solution)/shard_map/ppermute | solution.py:78
  222.7 230.6 %copy-start.3 = (bf16[512,2048]{1,0:T(8,128)(2,1)S(1)}, bf16[512,2048]{1,0:T(8,128)(2,1)}, u32[]{:S(2)}) copy-start(bf16[512,2048]{1,0:T(8,128)(2,1)} %param.9) | copy-start | bytes 6291460
Sparse Core Ops, SparseCore 0:
  17.2 40.9 all-reduce.1
  62.5 19.5 all-gather.5
  83.7 73.6 all-gather.7
  158.7 149.6 all-gather.3
  310.7 142.6 reduce-scatter.1
